TPU v7x, 256 devices: a whole 4x4x8 slice. The times are simulated.
256 devices in a mesh: gx: 32 (over y, x, core), gy: 8 (over z).
Axes of the slice: x: 4, y: 4, z: 8, core: 2. Of those that a mesh axis runs over, the one named last changes fastest.
Arguments:
- displacement: float32 [3, 32, 256, 1024], P(None, None, 'gx', 'gy'), may hold values from -6 to 6
- velocity: float32 [3, 32, 256, 1024], P(None, None, 'gx', 'gy'), may hold values from -6 to 6
- slopes: float32 [2, 32, 256, 1024], P(None, None, 'gx', 'gy'), may hold values from -0.5 to 0.5
- stretch: float32 [32, 256, 1024], P(None, 'gx', 'gy'), may hold values from 0.6 to 1.4
- moduli: float32 [2, 32, 256, 1024], P(None, None, 'gx', 'gy'), may hold values from 0.3 to 1
- buoyancy: float32 [32, 256, 1024], P(None, 'gx', 'gy'), may hold values from 0.5 to 1.5
- probes: float32 [4, 512, 128], P(None, 'gy'), may hold values from -0.0017089844 to 0.0017089844
Outputs:
- final_displacement: float32 [3, 32, 256, 1024], P(None, None, 'gx', 'gy')
- basis: float32 [128, 48, 128], P('gx', 'gy')
- factor: float32 [128, 128], replicated
All inputs are finite; a program needn't handle non-finite values.
Results may differ from a plain program's by a relative error of at most 0.0003.
Values sent between devices are 32-bit elements; how exact they have to be, the bound alone decides.
A program may use at most 64 MiB of HBM per device.

v0:
```python
import math
import jax
import jax.numpy as jnp
from jax import lax
from jax.sharding import PartitionSpec as P

STEPS = 4
time_step = 0.12


def extended(block, sides, width):
    for axis, dim in sides:
        count = lax.axis_size(axis)
        forward = [(i, i + 1) for i in range(count - 1)]
        backward = [(target, source) for source, target in forward]
        low = lax.ppermute(
            lax.slice_in_dim(block, block.shape[dim] - width, None, axis=dim), axis, forward
        )
        high = lax.ppermute(lax.slice_in_dim(block, 0, width, axis=dim), axis, backward)
        block = jnp.concatenate([low, block, high], axis=dim)
    return block


def fourth(values, dimension):
    length_out = values.shape[dimension] - 4

    def segment(offset):
        return lax.slice_in_dim(values, offset, offset + length_out, axis=dimension)

    return (segment(0) - segment(4) + 8.0 * (segment(3) - segment(1))) / 12.0


def vertical(values):
    padded = jnp.pad(values, ((0, 0), (2, 2), (0, 0), (0, 0)))
    return fourth(padded, 1)


def gradient(padded, slope_x, slope_y, stretch):
    d_x = fourth(padded[:, :, :, 2:-2], 2)
    d_y = fourth(padded[:, :, 2:-2, :], 3)
    d_r = vertical(padded[:, :, 2:-2, 2:-2])
    return jnp.stack([d_x + slope_x * d_r, d_y + slope_y * d_r, stretch * d_r], axis=1)


def stresses(gradients, lame, shear):
    divergence = gradients[0, 0] + gradients[1, 1] + gradients[2, 2]
    pressure = lame * divergence
    return jnp.stack(
        [
            pressure + 2.0 * shear * gradients[0, 0],
            pressure + 2.0 * shear * gradients[1, 1],
            pressure + 2.0 * shear * gradients[2, 2],
            shear * (gradients[0, 1] + gradients[1, 0]),
            shear * (gradients[0, 2] + gradients[2, 0]),
            shear * (gradients[1, 2] + gradients[2, 1]),
        ]
    )


def forces(padded, slope_x, slope_y, stretch):
    d_x = fourth(padded[:, :, :, 2:-2], 2)
    d_y = fourth(padded[:, :, 2:-2, :], 3)
    d_r = vertical(padded[:, :, 2:-2, 2:-2])
    rows_x = (0, 3, 4)
    rows_y = (3, 1, 5)
    rows_z = (4, 5, 2)
    return jnp.stack(
        [
            d_x[rows_x[component]]
            + slope_x * d_r[rows_x[component]]
            + d_y[rows_y[component]]
            + slope_y * d_r[rows_y[component]]
            + stretch * d_r[rows_z[component]]
            for component in range(3)
        ]
    )


def lower_factor(gram):
    order = gram.shape[0]
    positions = jnp.arange(order, dtype=jnp.int32)

    def column_step(column_index, lower):
        picker = (positions == column_index).astype(jnp.float32)
        column = jnp.dot(gram, picker, precision=lax.Precision.HIGHEST)
        row_of = jnp.dot(picker, lower, precision=lax.Precision.HIGHEST)
        column = column - jnp.dot(lower, row_of, precision=lax.Precision.HIGHEST)
        pivot = jnp.sqrt(jnp.sum(column * picker))
        entries = jnp.where(
            positions > column_index,
            column / pivot,
            jnp.where(positions == column_index, pivot, 0.0),
        )
        return lower + entries[:, None] * picker[None, :]

    return lax.fori_loop(0, order, column_step, jnp.zeros_like(gram))


def lower_inverse(lower):
    order = lower.shape[0]
    positions = jnp.arange(order, dtype=jnp.int32)

    def row_step(row_index, inverse):
        picker = (positions == row_index).astype(jnp.float32)
        row_of = jnp.dot(picker, lower, precision=lax.Precision.HIGHEST)
        pivot = jnp.sum(row_of * picker)
        fresh = (picker - jnp.dot(row_of, inverse, precision=lax.Precision.HIGHEST)) / pivot
        return inverse + picker[:, None] * fresh[None, :]

    return lax.fori_loop(0, order, row_step, jnp.zeros_like(lower))


def orthogonalize(tall_block, gram):
    lower = lower_factor(gram)
    inverse = lower_inverse(lower)
    result = jnp.dot(
        tall_block, inverse.T, precision=lax.Precision.HIGHEST, preferred_element_type=jnp.float32
    )
    return (result, lower.T)


def shards(displacement, velocity, slopes, stretch, moduli, buoyancy, probes):
    previous = displacement - time_step * velocity
    current = displacement
    for moment in range(STEPS):
        padded = extended(current, (("gx", 2), ("gy", 3)), 2)
        gradients = gradient(padded, slopes[0], slopes[1], stretch)
        stress = extended(stresses(gradients, moduli[0], moduli[1]), (("gx", 2), ("gy", 3)), 2)
        pushes = buoyancy * forces(stress, slopes[0], slopes[1], stretch)
        following = 2.0 * current - previous + time_step**2 * pushes
        velocities = (following - previous) / (2.0 * time_step)
        sampled = velocities[:, ::2, ::2, ::2]
        half_x = sampled.shape[2]
        rearranged = jnp.transpose(sampled, (2, 0, 1, 3)).reshape(-1, sampled.shape[3])
        sketch_term = jnp.dot(
            rearranged,
            probes[moment],
            precision=lax.Precision.HIGHEST,
            preferred_element_type=jnp.float32,
        ).reshape(half_x, -1, probes.shape[2])
        reduced = lax.psum_scatter(sketch_term, "gy", scatter_dimension=1, tiled=True)
        sketch = reduced if moment == 0 else sketch + reduced
        previous, current = (current, following)
    tall_block = sketch.reshape(-1, sketch.shape[2])
    rows_total = tall_block.shape[0] * lax.axis_size("gx") * lax.axis_size("gy")
    gram_local = jnp.dot(
        tall_block.T,
        tall_block,
        precision=lax.Precision.HIGHEST,
        preferred_element_type=jnp.float32,
    )
    gram_whole = lax.psum(gram_local, ("gx", "gy"))
    orthonormal, factor = orthogonalize(tall_block, gram_whole)
    basis = (math.sqrt(rows_total) * orthonormal).reshape(sketch.shape)
    return (current, basis, factor)


def solution(mesh):
    in_specs = (
        P(None, None, "gx", "gy"),
        P(None, None, "gx", "gy"),
        P(None, None, "gx", "gy"),
        P(None, "gx", "gy"),
        P(None, None, "gx", "gy"),
        P(None, "gx", "gy"),
        P(None, "gy", None),
    )
    out_specs = (P(None, None, "gx", "gy"), P("gx", "gy", None), P())
    return jax.shard_map(shards, mesh=mesh, in_specs=in_specs, out_specs=out_specs, check_vma=False)
```

profile of v0, /device:TPU:1, one launch (start us, length us, event | category | flops | bytes accessed | tf_op | source)
XLA Modules:
  0.0 1194.3 jit_solution(5939340690643367252)
XLA Ops:
  8.8 4.6 collective-permute-start
  13.4 2.0 collective-permute-start.1
  18.1 4.4 collective-permute-done.1
  26.6 4.9 collective-permute-start.2
  35.1 3.8 fusion.119
  42.7 1.8 fusion.162
  44.9 2.1 collective-permute-start.4
  47.0 2.2 collective-permute-start.5
  49.6 4.4 collective-permute-done.5
  56.2 2.4 copy.319
  59.1 3.6 collective-permute-start.6
  64.0 2.7 fusion.51
  69.5 2.4 copy.318
  71.9 3.0 fusion.94
  76.9 3.5 collective-permute-start.8
  80.4 1.9 collective-permute-start.9
  82.4 4.0 collective-permute-done.9
  89.0 3.7 collective-permute-start.10
  95.2 2.7 collective-permute-done.11
  99.3 2.1 fusion.155
  101.8 3.0 collective-permute-start.12
  104.8 1.9 collective-permute-start.13
  107.4 4.4 collective-permute-done.13
  111.8 1.8 fusion.291
  115.4 1.8 copy.329
  117.2 5.1 collective-permute-start.14
  125.4 2.5 collective-permute-done.15
  128.0 2.4 copy.332
  131.9 3.4 fusion.88
  136.6 2.9 collective-permute-start.16
  139.5 1.9 collective-permute-start.17
  141.4 6.0 slice.1072
  150.9 3.6 collective-permute-start.18
  157.0 2.4 collective-permute-done.19
  160.8 2.1 fusion.148
  163.3 5.1 collective-permute-start.20
  168.4 1.9 collective-permute-start.21
  171.9 6.0 slice.1074
  181.5 2.5 copy.342
  185.3 3.9 collective-permute-start.22
  190.5 2.7 fusion.41
  196.3 2.4 copy.341
  198.7 3.0 fusion.82
  202.2 5.1 collective-permute-start.24
  207.3 1.9 collective-permute-start.25
  210.9 2.5 slice.1076
  214.9 2.5 collective-permute-start.26
  220.1 2.0 collective-permute-done.27
  222.8 1.8 fusion.141
  225.0 5.1 collective-permute-start.28
  230.1 1.9 collective-permute-start.29
  233.0 4.0 collective-permute-done.29
  237.2 1.8 fusion.289
  239.0 2.4 copy.353
  243.1 3.7 collective-permute-start.30
  249.5 2.8 collective-permute-done.31
  252.3 2.4 copy.354
  254.7 2.4 copy.352
  257.1 3.4 fusion.76
  261.0 2.5 slice.1078
  266.5 78.0 %all-reduce.14.cloned.1.call-done = f32[4,48,128]{2,0,1:T(4,128)} async-done(((f32[4,48,128]{2,0,1:T(4,128)}), f32[4,48,128]{2,0,1:T(4,128)}) %all-reduce.14.cloned.1.call-update) | async-done | bytes 98320
  347.2 245.3 %all-reduce.12.cloned.1.call-done = f32[128,128]{1,0:T(8,128)} async-done(((f32[128,128]{1,0:T(8,128)}), f32[128,128]{1,0:T(8,128)}) %all-reduce.12.cloned.1.call-update) | async-done | bytes 65552 | tf_op jit(solution)/shard_map/psum | solution.py:152
  592.5 363.3 %while.30 = (s32[]{:T(128)}, f32[128,128]{1,0:T(8,128)S(1)}, f32[128,128]{1,0:T(8,128)}, s32[]{:T(128)}, s32[]{:T(128)}) while((s32[]{:T(128)}, f32[128,128]{1,0:T(8,128)S(1)}, f32[128,128]{1,0:T(8,128)}, s32[]{:T(128)}, s32[]{:T(128)}) %tuple.125), condition=%wide.region_7.8_spmd.clone.clone, body=%wide.region_5.7_spmd.clone.clone.sunk | while | flops 673410 | bytes 332917 | solution.py:96
  956.5 230.0 %while.29 = (s32[]{:T(128)}, f32[128,128]{1,0:T(8,128)S(1)}, f32[128,128]{1,0:T(8,128)S(1)}, s32[]{:T(128)}, s32[]{:T(128)}) while((s32[]{:T(128)}, f32[128,128]{1,0:T(8,128)S(1)}, f32[128,128]{1,0:T(8,128)S(1)}, s32[]{:T(128)}, s32[]{:T(128)}) %tuple.128), condition=%wide.region_10.11_spmd.clone, body=%wide.region_8.10_spmd.clone.sunk | while | flops 460034 | bytes 265316 | solution.py:110
  (1509 shorter events, 573.1 us)
Async XLA Ops:
  7.2 337.4 %all-reduce.14.cloned.1.call-start = ((), (), s32[]{:S(2)}) async-start(), calls=%async_computation.1 | async-start | bytes 196608
  8.7 6.7 copy-start.38
  8.7 6.7 copy-start.39
  8.7 6.8 copy-start.3
  8.8 7.5 copy-start.2
  8.8 9.3 collective-permute-start
  13.4 9.1 collective-permute-start.1
  15.5 29.0 %copy-start.4 = (f32[1,32,8,128]{3,2,1,0:T(8,128)}, f32[1,32,8,128]{3,2,1,0:T(8,128)S(1)}, u32[]{:S(2)}) copy-start(f32[1,32,8,128]{3,2,1,0:T(8,128)S(1)} %get-tuple-element.324) | copy-start | bytes 393220
  18.1 4.7 copy-start.23
  25.3 16.2 %collective-permute-start.3 = (f32[3,32,12,2]{1,3,2,0:T(2,128)}, f32[3,32,12,2]{1,3,2,0:T(2,128)}, u32[]{:S(2)}, u32[]{:S(2)}) collective-permute-start(f32[3,32,12,2]{1,3,2,0:T(2,128)} %get-tuple-element.276), channel_id=1, source_target_pairs={{1,0},{2,1},{3,2},{4,3},{5,4},{6,5},{7,6},{9,8},{10,9},{11,10},{12... | collective-permute-start | bytes 27656 | tf_op jit(solution)/shard_map/ppermute | solution.py:19
  26.6 12.3 %copy-start.1 = (f32[3,32,12,128]{1,3,2,0:T(8,128)S(1)}, f32[3,32,12,128]{1,3,2,0:T(8,128)}, u32[]{:S(2)}) copy-start(f32[3,32,12,128]{1,3,2,0:T(8,128)} %copy-done) | copy-start | bytes 1769476
  26.6 13.8 %collective-permute-start.2 = (f32[3,32,12,2]{1,3,2,0:T(2,128)}, f32[3,32,12,2]{1,3,2,0:T(2,128)}, u32[]{:S(2)}, u32[]{:S(2)}) collective-permute-start(f32[3,32,12,2]{1,3,2,0:T(2,128)} %get-tuple-element.277), channel_id=1, source_target_pairs={{0,1},{1,2},{2,3},{3,4},{4,5},{5,6},{6,7},{8,9},{9,10},{10,11},{11... | collective-permute-start | bytes 27656 | tf_op jit(solution)/shard_map/ppermute | solution.py:16
  40.4 2.2 copy-start.7
  40.4 2.2 copy-start.9
  40.4 2.2 copy-start.14
  44.7 4.5 copy-start.40
  44.9 4.7 collective-permute-start.4
  47.0 7.0 collective-permute-start.5
  49.6 4.4 copy-start.17
  59.1 10.4 collective-permute-start.6
  62.7 5.4 collective-permute-start.7
  71.9 3.0 copy-start.11
  71.9 3.0 copy-start.20
  76.9 5.5 collective-permute-start.8
  80.4 5.9 collective-permute-start.9
  86.4 7.7 copy-start.30
  89.0 9.1 collective-permute-start.10
  92.8 5.1 collective-permute-start.11
  95.2 4.1 copy-start.31
  101.8 5.6 collective-permute-start.12
  104.8 7.0 collective-permute-start.13
  117.2 13.2 %collective-permute-start.14 = (f32[6,32,12,2]{1,3,2,0:T(2,128)S(1)}, f32[6,32,12,2]{1,3,2,0:T(2,128)S(1)}, u32[]{:S(2)}, u32[]{:S(2)}) collective-permute-start(f32[6,32,12,2]{1,3,2,0:T(2,128)S(1)} %copy.329), channel_id=1, source_target_pairs={{0,1},{1,2},{2,3},{3,4},{4,5},{5,6},{6,7},{8,9},{9,10},{10,11},{11... | collective-permute-start | bytes 55304 | tf_op jit(solution)/shard_map/ppermute | solution.py:16
  122.3 5.7 collective-permute-start.15
  131.9 3.5 copy-start.12
  131.9 3.5 copy-start.21
  136.6 11.5 collective-permute-start.16
  139.5 8.6 collective-permute-start.17
  150.9 8.8 collective-permute-start.18
  154.5 4.8 collective-permute-start.19
  163.1 7.2 copy-start.33
  163.3 15.3 %collective-permute-start.20 = (f32[6,32,2,128]{3,1,2,0:T(8,128)S(1)}, f32[6,32,2,128]{3,1,2,0:T(8,128)S(1)}, u32[]{:S(2)}, u32[]{:S(2)}) collective-permute-start(f32[6,32,2,128]{3,1,2,0:T(8,128)S(1)} %get-tuple-element.294), channel_id=1, source_target_pairs={{0,8},{8,16},{16,24},{24,32},{32,40},{40,48},{48,56},{56,64},{64,7... | collective-permute-start | bytes 589832 | tf_op jit(solution)/shard_map/ppermute | solution.py:16
  168.4 10.2 collective-permute-start.21
  185.3 11.0 collective-permute-start.22
  189.3 5.7 collective-permute-start.23
  198.7 3.0 copy-start.13
  198.7 3.0 copy-start.22
  202.0 7.2 copy-start.34
  202.0 7.2 copy-start.36
  202.2 11.8 collective-permute-start.24
  207.3 6.7 collective-permute-start.25
  214.0 4.9 copy-start.29
  214.9 7.8 copy-start.8
  214.9 7.8 copy-start.10
  214.9 7.5 collective-permute-start.26
  217.4 4.7 collective-permute-start.27
  224.8 7.2 copy-start.35
  224.8 7.2 copy-start.37
  225.0 8.0 collective-permute-start.28
  230.1 7.0 collective-permute-start.29
  243.1 11.6 collective-permute-start.30
  246.9 5.4 collective-permute-start.31
  257.1 3.4 copy-start.19
  260.8 4.5 copy-start.41
  265.2 327.3 %all-reduce.12.cloned.1.call-start = ((), (), s32[]{:S(2)}) async-start(), calls=%async_computation | async-start | bytes 131072 | tf_op jit(solution)/shard_map/psum | solution.py:152
  (12 other events, 17.0 us)
Sparse Core Ops, SparseCore 0:
  265.3 79.1 all-reduce.13
  351.5 240.9 all-reduce.11
where the time goes:
time: 1210 us; the launch traced here: 1190 us
  matrix products  475 us (39%)
  waiting for transfers between devices  362 us (30%)
  loops' own time  98.3 us (8%)
  starting transfers between devices  89 us (7%)
  local copies, waits for them, and re-layouts  85.4 us (7%)
  other arithmetic  68.3 us (6%)
  between operations  15.9 us (1%)
    psum x1, waiting for transfers between devices, shards(): gram_whole = lax.psum(gram_local, ('gx', 'gy'))  245 us
    dot_general x128, matrix products, column_step(): column = jnp.dot(gram, picker, precision=lax.Precision.HIGHEST)  124 us
    dot_general x128, matrix products, column_step(): column = column - jnp.dot(lower, row_of, precision=lax.Precision.HIGHEST)  108 us
    dot_general x128, matrix products, row_step(): jnp.dot(row_of, inverse, precision=lax.Precision.HIGHEST)  107 us
    dot_general x128, matrix products, row_step(): row_of = jnp.dot(picker, lower, precision=lax.Precision.HIGHEST)  105 us
    another operation x1, loops' own time, lower_factor(): return lax.fori_loop(0, order, column_step, jnp.zeros_like(gram))  94 us
    unnamed x3, waiting for transfers between devices  78.1 us
    ppermute x16, starting transfers between devices, extended(): lax.ppermute(lax.slice_in_dim(block, block.shape[dim] - width, None, axis...  62.5 us
  transfers between devices with their start and end apart: 34, of which 17 were waited for; matrix products, arithmetic and copies ran while one was open for 5% of the time, Pallas kernels for 0%

commit v1 on v0

--- a/solution.py
+++ b/solution.py
@@ -149,7 +149,9 @@
         precision=lax.Precision.HIGHEST,
         preferred_element_type=jnp.float32,
     )
-    gram_whole = lax.psum(gram_local, ("gx", "gy"))
+    gram_whole = gram_local
+    for name in ("gx", "gy"):
+        gram_whole = lax.psum(gram_whole, name)
     orthonormal, factor = orthogonalize(tall_block, gram_whole)
     basis = (math.sqrt(rows_total) * orthonormal).reshape(sketch.shape)
     return (current, basis, factor)

time: 1210 us -> 1140 us (0.942)
  waiting for transfers between devices: 362 us -> 295 us
    psum x1 -> x2, waiting for transfers between devices: 245 us -> 178 us  [shards(): gram_whole = lax.psum(gram_whole, name)]
    unnamed x3 -> x4, waiting for transfers between devices: 78.1 us -> 78.1 us
  transfers between devices with their start and end apart: 34 -> 35, of which waited for: 17 -> 18; matrix products, arithmetic and copies ran while one was open for 5% -> 5% of each run, Pallas kernels for 0% -> 0%
where the time goes in v1:
time: 1140 us; the launch traced here: 1130 us
  matrix products  478 us (42%)
  waiting for transfers between devices  295 us (26%)
  loops' own time  97 us (9%)
  starting transfers between devices  89 us (8%)
  local copies, waits for them, and re-layouts  85.4 us (7%)
  other arithmetic  68.3 us (6%)
  between operations  15.6 us (1%)
    psum x2, waiting for transfers between devices, shards(): gram_whole = lax.psum(gram_whole, name)  178 us
    dot_general x128, matrix products, column_step(): column = jnp.dot(gram, picker, precision=lax.Precision.HIGHEST)  124 us
    dot_general x128, matrix products, column_step(): column = column - jnp.dot(lower, row_of, precision=lax.Precision.HIGHEST)  111 us
    dot_general x128, matrix products, row_step(): jnp.dot(row_of, inverse, precision=lax.Precision.HIGHEST)  107 us
    dot_general x128, matrix products, row_step(): row_of = jnp.dot(picker, lower, precision=lax.Precision.HIGHEST)  105 us
    another operation x1, loops' own time, lower_factor(): return lax.fori_loop(0, order, column_step, jnp.zeros_like(gram))  92.8 us
    unnamed x4, waiting for transfers between devices  78.1 us
    ppermute x16, starting transfers between devices, extended(): lax.ppermute(lax.slice_in_dim(block, block.shape[dim] - width, None, axis...  62.5 us
  transfers between devices with their start and end apart: 35, of which 18 were waited for; matrix products, arithmetic and copies ran while one was open for 5% of the time, Pallas kernels for 0%

profile of v1, /device:TPU:1, one launch (start us, length us, event | category | flops | bytes accessed | tf_op | source)
XLA Modules:
  0.0 1128.4 jit_solution(12860501427423339347)
XLA Ops:
  8.8 4.6 collective-permute-start
  13.4 2.0 collective-permute-start.1
  18.1 4.4 collective-permute-done.1
  26.6 4.9 collective-permute-start.2
  35.1 3.8 fusion.119
  42.7 1.8 fusion.162
  44.9 2.1 collective-permute-start.4
  47.0 2.2 collective-permute-start.5
  49.6 4.4 collective-permute-done.5
  56.2 2.4 copy.319
  59.1 3.6 collective-permute-start.6
  64.0 2.7 fusion.51
  69.5 2.4 copy.318
  71.9 3.0 fusion.94
  76.9 3.5 collective-permute-start.8
  80.4 1.9 collective-permute-start.9
  82.4 4.0 collective-permute-done.9
  89.0 3.7 collective-permute-start.10
  95.2 2.7 collective-permute-done.11
  99.3 2.1 fusion.155
  101.8 3.0 collective-permute-start.12
  104.8 1.9 collective-permute-start.13
  107.4 4.4 collective-permute-done.13
  111.8 1.8 fusion.291
  117.2 5.1 collective-permute-start.14
  125.4 2.5 collective-permute-done.15
  128.0 2.4 copy.332
  131.9 3.4 fusion.88
  136.6 2.9 collective-permute-start.16
  139.5 1.9 collective-permute-start.17
  141.4 6.0 slice.1072
  150.9 3.6 collective-permute-start.18
  157.0 2.4 collective-permute-done.19
  160.8 2.1 fusion.148
  163.3 5.1 collective-permute-start.20
  168.4 1.9 collective-permute-start.21
  171.9 6.0 slice.1074
  181.5 2.5 copy.342
  185.3 3.9 collective-permute-start.22
  190.5 2.7 fusion.41
  196.3 2.4 copy.341
  198.7 3.0 fusion.82
  202.2 5.1 collective-permute-start.24
  207.3 1.9 collective-permute-start.25
  210.9 2.5 slice.1076
  214.9 2.5 collective-permute-start.26
  220.1 2.0 collective-permute-done.27
  222.8 1.8 fusion.141
  225.0 5.1 collective-permute-start.28
  230.1 1.9 collective-permute-start.29
  233.0 4.0 collective-permute-done.29
  237.2 1.8 fusion.289
  239.0 2.4 copy.353
  243.1 3.7 collective-permute-start.30
  249.5 2.8 collective-permute-done.31
  252.3 2.4 copy.354
  254.7 2.4 copy.352
  257.1 3.4 fusion.76
  261.0 2.5 slice.1078
  266.5 78.0 %all-reduce.17.cloned.1.call-done = f32[4,48,128]{2,0,1:T(4,128)} async-done(((f32[4,48,128]{2,0,1:T(4,128)}), f32[4,48,128]{2,0,1:T(4,128)}) %all-reduce.17.cloned.1.call-update) | async-done | bytes 98320
  346.3 111.5 %all-reduce.13.cloned.1.call-done = f32[128,128]{1,0:T(8,128)} async-done(((f32[128,128]{1,0:T(8,128)}), f32[128,128]{1,0:T(8,128)}) %all-reduce.13.cloned.1.call-update) | async-done | bytes 65552 | tf_op jit(solution)/shard_map/psum | solution.py:154
  458.8 66.4 %all-reduce.15.cloned.1.call-done = f32[128,128]{1,0:T(8,128)} async-done(((f32[128,128]{1,0:T(8,128)}), f32[128,128]{1,0:T(8,128)}) %all-reduce.15.cloned.1.call-update) | async-done | bytes 65552 | tf_op jit(solution)/shard_map/psum | solution.py:154
  525.3 365.0 %while.30 = (s32[]{:T(128)}, f32[128,128]{1,0:T(8,128)S(1)}, f32[128,128]{1,0:T(8,128)}, s32[]{:T(128)}, s32[]{:T(128)}) while((s32[]{:T(128)}, f32[128,128]{1,0:T(8,128)S(1)}, f32[128,128]{1,0:T(8,128)}, s32[]{:T(128)}, s32[]{:T(128)}) %tuple.125), condition=%wide.region_8.9_spmd.clone.clone, body=%wide.region_6.8_spmd.clone.clone.sunk | while | flops 673410 | bytes 332917 | solution.py:96
  891.0 230.0 %while.29 = (s32[]{:T(128)}, f32[128,128]{1,0:T(8,128)S(1)}, f32[128,128]{1,0:T(8,128)S(1)}, s32[]{:T(128)}, s32[]{:T(128)}) while((s32[]{:T(128)}, f32[128,128]{1,0:T(8,128)S(1)}, f32[128,128]{1,0:T(8,128)S(1)}, s32[]{:T(128)}, s32[]{:T(128)}) %tuple.128), condition=%wide.region_11.12_spmd.clone, body=%wide.region_9.11_spmd.clone.sunk | while | flops 460034 | bytes 265316 | solution.py:110
  (1512 shorter events, 577.9 us)
Async XLA Ops:
  7.2 337.4 %all-reduce.17.cloned.1.call-start = ((), (), s32[]{:S(2)}) async-start(), calls=%async_computation.2 | async-start | bytes 196608
  8.7 6.7 copy-start.38
  8.7 6.7 copy-start.39
  8.7 6.8 copy-start.3
  8.8 7.5 copy-start.2
  8.8 9.3 collective-permute-start
  13.4 9.1 collective-permute-start.1
  15.5 29.0 %copy-start.4 = (f32[1,32,8,128]{3,2,1,0:T(8,128)}, f32[1,32,8,128]{3,2,1,0:T(8,128)S(1)}, u32[]{:S(2)}) copy-start(f32[1,32,8,128]{3,2,1,0:T(8,128)S(1)} %get-tuple-element.324) | copy-start | bytes 393220
  18.1 4.7 copy-start.23
  25.3 16.2 %collective-permute-start.3 = (f32[3,32,12,2]{1,3,2,0:T(2,128)}, f32[3,32,12,2]{1,3,2,0:T(2,128)}, u32[]{:S(2)}, u32[]{:S(2)}) collective-permute-start(f32[3,32,12,2]{1,3,2,0:T(2,128)} %get-tuple-element.276), channel_id=1, source_target_pairs={{1,0},{2,1},{3,2},{4,3},{5,4},{6,5},{7,6},{9,8},{10,9},{11,10},{12... | collective-permute-start | bytes 27656 | tf_op jit(solution)/shard_map/ppermute | solution.py:19
  26.6 12.3 %copy-start.1 = (f32[3,32,12,128]{1,3,2,0:T(8,128)S(1)}, f32[3,32,12,128]{1,3,2,0:T(8,128)}, u32[]{:S(2)}) copy-start(f32[3,32,12,128]{1,3,2,0:T(8,128)} %copy-done) | copy-start | bytes 1769476
  26.6 13.8 %collective-permute-start.2 = (f32[3,32,12,2]{1,3,2,0:T(2,128)}, f32[3,32,12,2]{1,3,2,0:T(2,128)}, u32[]{:S(2)}, u32[]{:S(2)}) collective-permute-start(f32[3,32,12,2]{1,3,2,0:T(2,128)} %get-tuple-element.277), channel_id=1, source_target_pairs={{0,1},{1,2},{2,3},{3,4},{4,5},{5,6},{6,7},{8,9},{9,10},{10,11},{11... | collective-permute-start | bytes 27656 | tf_op jit(solution)/shard_map/ppermute | solution.py:16
  40.4 2.2 copy-start.9
  40.4 2.2 copy-start.14
  44.7 4.5 copy-start.40
  44.9 4.7 collective-permute-start.4
  47.0 7.0 collective-permute-start.5
  49.6 4.4 copy-start.17
  59.1 10.4 collective-permute-start.6
  62.7 5.4 collective-permute-start.7
  71.9 3.0 copy-start.11
  71.9 3.0 copy-start.20
  76.9 5.5 collective-permute-start.8
  80.4 5.9 collective-permute-start.9
  86.4 7.7 copy-start.30
  89.0 9.1 collective-permute-start.10
  92.8 5.1 collective-permute-start.11
  95.2 4.1 copy-start.31
  101.8 5.6 collective-permute-start.12
  104.8 7.0 collective-permute-start.13
  117.2 13.2 %collective-permute-start.14 = (f32[6,32,12,2]{1,3,2,0:T(2,128)S(1)}, f32[6,32,12,2]{1,3,2,0:T(2,128)S(1)}, u32[]{:S(2)}, u32[]{:S(2)}) collective-permute-start(f32[6,32,12,2]{1,3,2,0:T(2,128)S(1)} %copy.329), channel_id=1, source_target_pairs={{0,1},{1,2},{2,3},{3,4},{4,5},{5,6},{6,7},{8,9},{9,10},{10,11},{11... | collective-permute-start | bytes 55304 | tf_op jit(solution)/shard_map/ppermute | solution.py:16
  122.3 5.7 collective-permute-start.15
  131.9 3.5 copy-start.12
  131.9 3.5 copy-start.21
  136.6 11.5 %collective-permute-start.16 = (f32[3,32,2,128]{3,1,2,0:T(8,128)S(1)}, f32[3,32,2,128]{3,1,2,0:T(8,128)S(1)}, u32[]{:S(2)}, u32[]{:S(2)}) collective-permute-start(f32[3,32,2,128]{3,1,2,0:T(8,128)S(1)} %get-tuple-element.316), channel_id=1, source_target_pairs={{0,8},{8,16},{16,24},{24,32},{32,40},{40,48},{48,56},{56,64},{64,7... | collective-permute-start | bytes 294920 | tf_op jit(solution)/shard_map/ppermute | solution.py:16
  139.5 8.6 collective-permute-start.17
  150.9 8.8 collective-permute-start.18
  154.5 4.8 collective-permute-start.19
  163.1 7.2 copy-start.33
  163.3 15.3 %collective-permute-start.20 = (f32[6,32,2,128]{3,1,2,0:T(8,128)S(1)}, f32[6,32,2,128]{3,1,2,0:T(8,128)S(1)}, u32[]{:S(2)}, u32[]{:S(2)}) collective-permute-start(f32[6,32,2,128]{3,1,2,0:T(8,128)S(1)} %get-tuple-element.294), channel_id=1, source_target_pairs={{0,8},{8,16},{16,24},{24,32},{32,40},{40,48},{48,56},{56,64},{64,7... | collective-permute-start | bytes 589832 | tf_op jit(solution)/shard_map/ppermute | solution.py:16
  168.4 10.2 collective-permute-start.21
  185.3 11.0 collective-permute-start.22
  189.3 5.7 collective-permute-start.23
  198.7 3.0 copy-start.13
  198.7 3.0 copy-start.22
  202.0 7.2 copy-start.34
  202.0 7.2 copy-start.36
  202.2 11.8 %collective-permute-start.24 = (f32[3,32,2,128]{3,1,2,0:T(8,128)S(1)}, f32[3,32,2,128]{3,1,2,0:T(8,128)S(1)}, u32[]{:S(2)}, u32[]{:S(2)}) collective-permute-start(f32[3,32,2,128]{3,1,2,0:T(8,128)S(1)} %get-tuple-element.312), channel_id=1, source_target_pairs={{0,8},{8,16},{16,24},{24,32},{32,40},{40,48},{48,56},{56,64},{64,7... | collective-permute-start | bytes 294920 | tf_op jit(solution)/shard_map/ppermute | solution.py:16
  207.3 6.7 collective-permute-start.25
  214.0 4.9 copy-start.29
  214.9 7.8 copy-start.8
  214.9 7.8 copy-start.10
  214.9 7.5 collective-permute-start.26
  217.4 4.7 collective-permute-start.27
  224.8 7.2 copy-start.35
  224.8 7.2 copy-start.37
  225.0 8.0 collective-permute-start.28
  230.1 7.0 collective-permute-start.29
  243.1 11.6 %collective-permute-start.30 = (f32[6,32,12,2]{1,3,2,0:T(2,128)S(1)}, f32[6,32,12,2]{1,3,2,0:T(2,128)}, u32[]{:S(2)}, u32[]{:S(2)}) collective-permute-start(f32[6,32,12,2]{1,3,2,0:T(2,128)S(1)} %copy.351), channel_id=1, source_target_pairs={{0,1},{1,2},{2,3},{3,4},{4,5},{5,6},{6,7},{8,9},{9,10},{10,11},{11... | collective-permute-start | bytes 55304 | tf_op jit(solution)/shard_map/ppermute | solution.py:16
  246.9 5.4 collective-permute-start.31
  257.1 3.4 copy-start.19
  260.8 4.5 copy-start.41
  265.2 192.6 %all-reduce.13.cloned.1.call-start = ((), (), s32[]{:S(2)}) async-start(), calls=%async_computation | async-start | bytes 131072 | tf_op jit(solution)/shard_map/psum | solution.py:154
  346.2 179.0 %all-reduce.15.cloned.1.call-start = ((), (), s32[]{:S(2)}) async-start(), calls=%async_computation.1 | async-start | bytes 131072 | tf_op jit(solution)/shard_map/psum | solution.py:154
  (13 other events, 19.2 us)
Sparse Core Ops, SparseCore 0:
  265.3 79.1 all-reduce.16
  348.7 109.0 all-reduce.12
  460.1 65.1 all-reduce.14
